TPU v7x, 256 devices: a whole 4x4x8 slice. The times are simulated.
256 devices in a mesh: dp: 32 (over x, z), ctx: 8 (over y, core).
Axes of the slice: x: 4, y: 4, z: 8, core: 2. Of those that a mesh axis runs over, the one named last changes fastest.
Arguments:
- hidden: bfloat16 [32, 2048, 4096], P('dp', 'ctx'), may hold values from -6 to 6
- segments: int32 [32, 2048], P('dp', 'ctx'), may hold values from 0 to 15, as said below
- gain: float32 [4096], replicated, may hold values from 0.25 to 1.75
- inv_temp: float32 [], replicated, may hold values from 20 to 50
- positives: int32 [512], P(('dp', 'ctx')), may hold values from 0 to 511, as said below
Outputs:
- grad_hidden: bfloat16 [32, 2048, 4096], P('dp', 'ctx')
- grad_gain: float32 [4096], replicated
- loss: float32 [], replicated
Inputs may be any that keep to these rules, and one draw needn't show every extreme that they name: `segments`: in each sequence the document numbers never fall along positions and every document has one position or more; document 0 covers more than half of the sequence's positions. `positives`: no document is its own positive.
All inputs are finite; a program needn't handle non-finite values.
Results may differ from a plain program's by a relative error of at most 0.0053.
Values may be sent and summed in bfloat16 or wider, within the bound.
A program may use at most 64 MiB of HBM per device.

v0:
```python
import jax
import jax.numpy as jnp
from jax import lax
from jax.sharding import PartitionSpec as P

DOCS_DEV = 2


def normalize_docs(pooled_totals, counts):
    pooled = pooled_totals / counts[:, None]
    rnorm = lax.rsqrt(jnp.sum(pooled * pooled, axis=-1, keepdims=True) + 1e-06)
    return (pooled * rnorm, rnorm)


def body(hidden, segments, gain, inv_temp, positives):
    states = hidden[0].astype(jnp.float32)
    scale_t = lax.rsqrt(jnp.mean(states * states, axis=-1, keepdims=True) + 1e-06)
    normalized_rows = states * scale_t * gain
    ctx_count = lax.axis_size("ctx")
    seq_docs = DOCS_DEV * ctx_count
    document_indicator = (
        segments[0][:, None] == jnp.arange(seq_docs, dtype=jnp.int32)[None, :]
    ).astype(jnp.float32)
    pooled_totals = lax.dot_general(
        document_indicator,
        normalized_rows,
        (((0,), (0,)), ((), ())),
        precision=lax.Precision.HIGHEST,
    )
    counts = jnp.sum(document_indicator, axis=0)
    ctx_rank = lax.axis_index("ctx")
    own_sums, own_counts = (
        lax.psum_scatter(pooled_totals, "ctx", scatter_dimension=0, tiled=True),
        lax.psum_scatter(counts, "ctx", scatter_dimension=0, tiled=True),
    )
    emb_f, rnorm = normalize_docs(own_sums, own_counts)
    emb_own = emb_f.astype(jnp.bfloat16)
    emb_all = lax.all_gather(emb_own, ("dp", "ctx"), axis=0, tiled=True)
    all_docs = emb_all.shape[0]
    row_first = (lax.axis_index("dp") * ctx_count + ctx_rank) * DOCS_DEV
    logits = (
        lax.dot_general(
            emb_own, emb_all, (((1,), (1,)), ((), ())), preferred_element_type=jnp.float32
        )
        * inv_temp
    )
    columns = jnp.arange(all_docs, dtype=jnp.int32)[None, :]
    own_rows = row_first + jnp.arange(DOCS_DEV, dtype=jnp.int32)[:, None]
    pos_mask = (columns == positives[:, None]).astype(jnp.float32)
    logits = jnp.where(columns == own_rows, -1e30, logits)
    top = jnp.max(logits, axis=1, keepdims=True)
    expo = jnp.exp(logits - top)
    total = jnp.sum(expo, axis=1, keepdims=True)
    lse = top[:, 0] + jnp.log(total[:, 0])
    loss_local = jnp.sum(lse - jnp.sum(pos_mask * logits, axis=1)) / all_docs
    gmat = ((expo / total - pos_mask) * (inv_temp / all_docs)).astype(jnp.bfloat16)
    row_grad = jnp.dot(gmat, emb_all, preferred_element_type=jnp.float32)
    grad_rows = lax.all_gather(gmat, ("dp", "ctx"), axis=0, tiled=True)
    grad_cols = lax.dynamic_slice_in_dim(grad_rows, row_first, DOCS_DEV, 1)
    col_grad = lax.dot_general(
        grad_cols, emb_all, (((0,), (0,)), ((), ())), preferred_element_type=jnp.float32
    )
    demb = row_grad + col_grad
    dpool = rnorm * (demb - emb_f * jnp.sum(emb_f * demb, axis=-1, keepdims=True))
    dsum_own = dpool / own_counts[:, None]
    dsum_seq = lax.all_gather(dsum_own, "ctx", axis=0, tiled=True)
    normalized_gradient = jnp.dot(document_indicator, dsum_seq, precision=lax.Precision.HIGHEST)
    gain_local = jnp.sum(normalized_gradient * states * scale_t, axis=0)
    grad_gain, loss = lax.psum((gain_local, loss_local), ("dp", "ctx"))
    grad_out = normalized_gradient * gain
    inner = jnp.mean(grad_out * states, axis=-1, keepdims=True)
    grad_hidden = (scale_t * grad_out - states * scale_t**3 * inner).astype(jnp.bfloat16)
    return (grad_hidden[None], grad_gain, loss)


def solution(mesh):
    return jax.shard_map(
        body,
        mesh=mesh,
        in_specs=(P("dp", "ctx", None), P("dp", "ctx"), P(), P(), P(("dp", "ctx"))),
        out_specs=(P("dp", "ctx", None), P(), P()),
        check_vma=False,
    )
```

profile of v0, /device:TPU:1, one launch (start us, length us, event | category | flops | bytes accessed | tf_op | source)
XLA Modules:
  0.0 389.6 jit_solution(4266364074889755771)
XLA Ops:
  7.2 2.1 fusion
  9.3 4.2 %fusion.2 = f32[16,4096]{1,0:T(8,128)} fusion(bf16[1,256,4096]{2,1,0:T(8,128)(2,1)} %param.5, f32[4096]{0:T(1024)} %param.7, f32[256]{0:T(256)S(1)} %get-tuple-element.12, s32[256]{0:T(256)} %bitcast.26), kind=kOutput, calls=%fused_computation.8 | convolution fusion | flops 204476416 | bytes 2377728 | tf_op jit(solution)/shard_map/dot_general | solution.py:24
  13.6 0.6 dynamic-slice
  14.8 0.1 convert_reduce_fusion
  15.0 15.0 %all-reduce.1 = f32[16]{0:T(128)S(1)} all-reduce(f32[16]{0:T(128)S(1)} %convert_reduce_fusion), channel_id=3, replica_groups=mesh['dp'=32,'ctx'=8] {'ctx'}, use_global_device_ids=true, to_apply=%region_3.0.clone | all-reduce | flops 16 | bytes 128
  30.0 50.8 %all-reduce.5.cloned.1.call-done = f32[16,4096]{1,0:T(8,128)} async-done(((f32[16,4096]{1,0:T(8,128)}), f32[16,4096]{1,0:T(8,128)}) %all-reduce.5.cloned.1.call-update) | async-done | bytes 262160
  80.8 1.1 multiply_reduce_fusion.1
  81.9 0.7 fusion.30
  83.3 119.1 %all-gather.5.cloned.1.call-done = bf16[256,2,4096]{2,1,0:T(2,128)(2,1)} async-done(((bf16[1,2,4096]{2,1,0:T(2,128)(2,1)}), bf16[256,2,4096]{2,1,0:T(2,128)(2,1)}) %all-gather.5.cloned.1.call-update) | async-done | bytes 4194320 | tf_op jit(solution)/shard_map/all_gather | solution.py:38
  202.4 7.2 %reshape.46 = bf16[512,4096]{1,0:T(8,128)(2,1)} reshape(bf16[256,2,4096]{2,1,0:T(2,128)(2,1)} %all-gather.5.cloned.1.call-done) | data formatting | bytes 8388608
  209.6 3.6 fusion.21
  213.3 0.2 select_reduce_fusion
  213.5 0.1 fusion.29
  213.6 0.7 fusion.22
  214.3 0.6 subtract_reduce_fusion
  215.6 67.0 %all-gather.1 = bf16[256,2,512]{2,1,0:T(2,128)(2,1)S(1)} all-gather(bf16[1,2,512]{2,1,0:T(2,128)(2,1)S(1)} %fusion.29), channel_id=1, replica_groups=mesh['dp'=32,'ctx'=8] {'dp','ctx'}, dimensions={0}, use_global_device_ids=true | all-gather | bytes 526336 | tf_op jit(solution)/shard_map/all_gather | solution.py:58
  282.6 0.2 reshape.48
  282.8 3.1 multiply_reduce_fusion
  285.9 0.1 divide_bitcast_fusion
  286.0 12.8 %all-gather.2 = f32[8,2,4096]{2,1,0:T(2,128)S(1)} all-gather(f32[1,2,4096]{2,1,0:T(2,128)S(1)} %divide_bitcast_fusion), channel_id=1, replica_groups=mesh['dp'=32,'ctx'=8] {'ctx'}, dimensions={0}, use_global_device_ids=true | all-gather | bytes 294912 | tf_op jit(solution)/shard_map/all_gather | solution.py:66
  298.8 0.2 reshape.50
  299.0 4.8 %fusion.9 = (f32[4096]{0:T(1024)S(1)}, f32[256]{0:T(256)S(1)}, f32[256,4096]{1,0:T(8,128)}) fusion(bf16[1,256,4096]{2,1,0:T(8,128)(2,1)S(1)} %copy-done.1, f32[256]{0:T(256)S(1)} %get-tuple-element.12, f32[4096]{0:T(1024)S(1)} %copy-done.2, f32[16,4096]{1,0:T(8,128)S(1)} %reshape.50, s32[256]{0:T(256)S(1)} %bitcast.28), kind=kOutput, calls=%fused_computation.14 | convolution fusion | flops 208666368 | bytes 6589440 | tf_op jit(solution)/shard_map/dot_general | solution.py:67
  303.8 74.0 %all-reduce.2 = (f32[4096]{0:T(1024)}, f32[]{:T(128)}) all-reduce(f32[4096]{0:T(1024)S(1)} %get-tuple-element.3, f32[]{:T(128)S(6)} %div.42), channel_id=1, replica_groups=mesh['dp'=32,'ctx'=8] {'dp','ctx'}, use_global_device_ids=true, to_apply=%region_10.11 | all-reduce | flops 4097 | bytes 32776 | tf_op jit(solution)/shard_map/psum | solution.py:69
  377.8 5.0 %fusion.10 = bf16[1,256,4096]{2,1,0:T(8,128)(2,1)} fusion(f32[256,4096]{1,0:T(8,128)} %get-tuple-element.17, bf16[1,256,4096]{2,1,0:T(8,128)(2,1)S(1)} %copy-done.1, f32[256]{0:T(256)S(1)} %broadcast_multiply_fusion, f32[256]{0:T(256)S(1)} %get-tuple-element.11, f32[4096]{0:T(1024)S(1)} %copy-done.2, f32[256]{0:T(256)S(1)} %get-tuple-element.12), kind=kLoop, calls=%fused_computation.15 | loop fusion | flops 7340032 | bytes 8408064 | tf_op jit(solution)/shard_map/broadcast_in_dim | solution.py:73
  (21 shorter events, 0.2 us)
Async XLA Ops:
  7.2 6.4 %copy-start.5 = (u32[256]{0:T(256)S(1)}, u32[256]{0:T(256)}, u32[]{:S(2)}) copy-start(u32[256]{0:T(256)} %constant.40) | copy-start | bytes 3076
  7.2 7.7 %copy-start.4 = (s32[1,256]{1,0:T(1,128)S(1)}, s32[1,256]{1,0:T(1,128)}, u32[]{:S(2)}) copy-start(s32[1,256]{1,0:T(1,128)} %param.6) | copy-start | bytes 3076
  7.2 73.6 %all-reduce.5.cloned.1.call-start = ((), (), s32[]{:S(2)}) async-start(), calls=%async_computation.1 | async-start | bytes 524288
  13.5 188.9 %all-gather.5.cloned.1.call-start = ((), (), s32[]{:S(2)}) async-start(), calls=%async_computation | async-start | bytes 4210688 | tf_op jit(solution)/shard_map/all_gather | solution.py:38
  209.6 3.6 copy-start.3
  209.6 4.0 %copy-start = (bf16[512,4096]{1,0:T(8,128)(2,1)S(1)}, bf16[512,4096]{1,0:T(8,128)(2,1)}, u32[]{:S(2)}) copy-start(bf16[512,4096]{1,0:T(8,128)(2,1)} %reshape.46) | copy-start | bytes 12582916
  214.3 84.7 %copy-start.1 = (bf16[1,256,4096]{2,1,0:T(8,128)(2,1)S(1)}, bf16[1,256,4096]{2,1,0:T(8,128)(2,1)}, u32[]{:S(2)}) copy-start(bf16[1,256,4096]{2,1,0:T(8,128)(2,1)} %param.5) | copy-start | bytes 6291460
  214.3 84.7 %copy-start.2 = (f32[4096]{0:T(1024)S(1)}, f32[4096]{0:T(1024)}, u32[]{:S(2)}) copy-start(f32[4096]{0:T(1024)} %param.7) | copy-start | bytes 49156
Sparse Core Ops, SparseCore 0:
  13.7 67.1 all-reduce.4
  85.1 117.3 all-gather.4
where the time goes:
time: 390 us
  waiting for transfers between devices  170 us (44%)
  blocking collectives  169 us (43%)
  matrix products  16.3 us (4%)
  between operations  16.1 us (4%)
  other arithmetic  10 us (3%)
  local copies, waits for them, and re-layouts  8.27 us (2%)
    all_gather x1, waiting for transfers between devices, body(): emb_all = lax.all_gather(emb_own, ('dp', 'ctx'), axis=0, tiled=True)  119 us
    psum x1, blocking collectives, body(): grad_gain, loss = lax.psum((gain_local, loss_local), ('dp', 'ctx'))  74 us
    all_gather x1, blocking collectives, body(): grad_rows = lax.all_gather(gmat, ('dp', 'ctx'), axis=0, tiled=True)  67 us
    unnamed x3, waiting for transfers between devices  50.8 us
    unnamed x1, blocking collectives  15 us
    all_gather x1, blocking collectives, body(): dsum_seq = lax.all_gather(dsum_own, 'ctx', axis=0, tiled=True)  12.8 us
    unnamed x17, local copies, waits for them, and re-layouts  8.27 us
  transfers between devices with their start and end apart: 2, of which 2 were waited for; matrix products, arithmetic and copies ran while one was open for 0% of the time, Pallas kernels for 0%

commit v1 on v0

--- a/solution.py
+++ b/solution.py
@@ -55,7 +55,10 @@
     loss_local = jnp.sum(lse - jnp.sum(pos_mask * logits, axis=1)) / all_docs
     gmat = ((expo / total - pos_mask) * (inv_temp / all_docs)).astype(jnp.bfloat16)
     row_grad = jnp.dot(gmat, emb_all, preferred_element_type=jnp.float32)
-    grad_rows = lax.all_gather(gmat, ("dp", "ctx"), axis=0, tiled=True)
+    grad_rows = jnp.concatenate(
+        lax.all_to_all(jnp.stack([gmat] * lax.axis_size(("dp", "ctx"))), ("dp", "ctx"), 0, 0),
+        axis=0,
+    )
     grad_cols = lax.dynamic_slice_in_dim(grad_rows, row_first, DOCS_DEV, 1)
     col_grad = lax.dot_general(
         grad_cols, emb_all, (((0,), (0,)), ((), ())), preferred_element_type=jnp.float32

time: 390 us -> 351 us (0.900)
  blocking collectives: 169 us -> 101 us
  waiting for transfers between devices: 170 us -> 186 us
  starting transfers between devices: 0.08 us -> 8.92 us
    all_gather x1 -> x0, blocking collectives: 67 us -> none  [body(): grad_rows = lax.all_gather(gmat, ('dp', 'ctx'), axis=0, tiled=True)]
    all_to_all x0 -> x1, waiting for transfers between devices: none -> 16.4 us  [body(): lax.all_to_all(jnp.stack([gmat] * lax.axis_size(('dp', 'ctx'))), ('dp', '...]
    all_to_all x0 -> x1, starting transfers between devices: none -> 8.84 us  [body(): lax.all_to_all(jnp.stack([gmat] * lax.axis_size(('dp', 'ctx'))), ('dp', '...]
    unnamed x17 -> x14, local copies, waits for them, and re-layouts: 8.27 us -> 8.07 us
  transfers between devices with their start and end apart: 2 -> 3, of which waited for: 2 -> 3; matrix products, arithmetic and copies ran while one was open for 0% -> 1% of each run, Pallas kernels for 0% -> 0%
where the time goes in v1:
time: 351 us; the launch traced here: 350 us
  waiting for transfers between devices  186 us (53%)
  blocking collectives  101 us (29%)
  matrix products  18.3 us (5%)
  between operations  16.1 us (5%)
  other arithmetic  10 us (3%)
  local copies, waits for them, and re-layouts  9.33 us (3%)
  starting transfers between devices  8.92 us (3%)
    all_gather x1, waiting for transfers between devices, body(): emb_all = lax.all_gather(emb_own, ('dp', 'ctx'), axis=0, tiled=True)  119 us
    psum x1, blocking collectives, body(): grad_gain, loss = lax.psum((gain_local, loss_local), ('dp', 'ctx'))  73.4 us
    unnamed x3, waiting for transfers between devices  50.8 us
    all_to_all x1, waiting for transfers between devices, body(): lax.all_to_all(jnp.stack([gmat] * lax.axis_size(('dp', 'ctx'))), ('dp', '...  16.4 us
    unnamed x1, blocking collectives  15 us
    all_gather x1, blocking collectives, body(): dsum_seq = lax.all_gather(dsum_own, 'ctx', axis=0, tiled=True)  12.6 us
    all_to_all x1, starting transfers between devices, body(): lax.all_to_all(jnp.stack([gmat] * lax.axis_size(('dp', 'ctx'))), ('dp', '...  8.84 us
    unnamed x14, local copies, waits for them, and re-layouts  8.07 us
  transfers between devices with their start and end apart: 3, of which 3 were waited for; matrix products, arithmetic and copies ran while one was open for 1% of the time, Pallas kernels for 0%

profile of v1, /device:TPU:1, one launch (start us, length us, event | category | flops | bytes accessed | tf_op | source)
XLA Modules:
  0.0 350.1 jit_solution(13982006114123147995)
XLA Ops:
  7.2 2.1 fusion
  9.3 4.2 %fusion.2 = f32[16,4096]{1,0:T(8,128)} fusion(bf16[1,256,4096]{2,1,0:T(8,128)(2,1)} %param.5, f32[4096]{0:T(1024)} %param.7, f32[256]{0:T(256)S(1)} %get-tuple-element.12, s32[256]{0:T(256)} %bitcast.24), kind=kOutput, calls=%fused_computation.8 | convolution fusion | flops 204476416 | bytes 2377728 | tf_op jit(solution)/shard_map/dot_general | solution.py:24
  13.6 0.6 dynamic-slice
  14.8 0.1 convert_reduce_fusion
  15.0 15.0 %all-reduce.1 = f32[16]{0:T(128)S(1)} all-reduce(f32[16]{0:T(128)S(1)} %convert_reduce_fusion), channel_id=3, replica_groups=mesh['dp'=32,'ctx'=8] {'ctx'}, use_global_device_ids=true, to_apply=%region_3.0.clone | all-reduce | flops 16 | bytes 128
  30.0 50.8 %all-reduce.5.cloned.1.call-done = f32[16,4096]{1,0:T(8,128)} async-done(((f32[16,4096]{1,0:T(8,128)}), f32[16,4096]{1,0:T(8,128)}) %all-reduce.5.cloned.1.call-update) | async-done | bytes 262160
  80.8 1.1 multiply_reduce_fusion.1
  82.0 0.7 fusion.29
  83.3 119.1 %all-gather.4.cloned.1.call-done = bf16[256,2,4096]{2,1,0:T(2,128)(2,1)} async-done(((bf16[1,2,4096]{2,1,0:T(2,128)(2,1)}), bf16[256,2,4096]{2,1,0:T(2,128)(2,1)}) %all-gather.4.cloned.1.call-update) | async-done | bytes 4194320 | tf_op jit(solution)/shard_map/all_gather | solution.py:38
  202.4 7.2 %reshape.52 = bf16[512,4096]{1,0:T(8,128)(2,1)} reshape(bf16[256,2,4096]{2,1,0:T(2,128)(2,1)} %all-gather.4.cloned.1.call-done) | data formatting | bytes 8388608
  209.6 3.5 fusion.21
  213.2 0.2 select_reduce_fusion
  213.5 1.1 stack.2
  214.5 8.8 %all-to-all-start = ((bf16[256,2,512]{2,1,0:T(2,128)(2,1)}), bf16[256,2,512]{2,1,0:T(2,128)(2,1)S(1)}, u32[]{:S(2)}, u32[]{:S(2)}) async-start(bf16[256,2,512]{2,1,0:T(2,128)(2,1)} %stack.2), calls=%async_computation | async-start | bytes 1048576 | tf_op jit(solution)/shard_map/all_to_all | solution.py:59
  223.4 0.6 subtract_reduce_fusion
  224.6 2.8 fusion.22
  227.5 16.4 %all-to-all-done = bf16[256,2,512]{2,1,0:T(2,128)(2,1)S(1)} async-done(((bf16[256,2,512]{2,1,0:T(2,128)(2,1)}), bf16[256,2,512]{2,1,0:T(2,128)(2,1)S(1)}, u32[]{:S(2)}, u32[]{:S(2)}) %all-to-all-start) | async-done | bytes 524320 | tf_op jit(solution)/shard_map/all_to_all | solution.py:59
  243.9 0.2 reshape.49
  244.1 3.1 multiply_reduce_fusion
  247.3 12.6 %all-gather.1 = f32[8,2,4096]{2,1,0:T(2,128)S(1)} all-gather(f32[1,2,4096]{2,1,0:T(2,128)S(1)} %divide_bitcast_fusion), channel_id=1, replica_groups=mesh['dp'=32,'ctx'=8] {'ctx'}, dimensions={0}, use_global_device_ids=true | all-gather | bytes 294912 | tf_op jit(solution)/shard_map/all_gather | solution.py:69
  259.9 0.2 reshape.54
  260.1 4.8 %fusion.9 = (f32[4096]{0:T(1024)S(1)}, f32[256]{0:T(256)S(1)}, f32[256,4096]{1,0:T(8,128)}) fusion(bf16[1,256,4096]{2,1,0:T(8,128)(2,1)S(1)} %copy-done, f32[256]{0:T(256)S(1)} %get-tuple-element.12, f32[4096]{0:T(1024)S(1)} %copy-done.1, f32[16,4096]{1,0:T(8,128)S(1)} %reshape.54, s32[256]{0:T(256)S(1)} %bitcast.26), kind=kOutput, calls=%fused_computation.14 | convolution fusion | flops 208666368 | bytes 6589440 | tf_op jit(solution)/shard_map/dot_general | solution.py:70
  264.9 73.4 %all-reduce.2 = (f32[4096]{0:T(1024)}, f32[]{:T(128)}) all-reduce(f32[4096]{0:T(1024)S(1)} %get-tuple-element.3, f32[]{:T(128)S(6)} %div.42), channel_id=1, replica_groups=mesh['dp'=32,'ctx'=8] {'dp','ctx'}, use_global_device_ids=true, to_apply=%region_10.11 | all-reduce | flops 4097 | bytes 32776 | tf_op jit(solution)/shard_map/psum | solution.py:72
  338.3 5.0 %fusion.10 = bf16[1,256,4096]{2,1,0:T(8,128)(2,1)} fusion(f32[256,4096]{1,0:T(8,128)} %get-tuple-element.17, bf16[1,256,4096]{2,1,0:T(8,128)(2,1)S(1)} %copy-done, f32[256]{0:T(256)S(1)} %broadcast_multiply_fusion, f32[256]{0:T(256)S(1)} %get-tuple-element.11, f32[4096]{0:T(1024)S(1)} %copy-done.1, f32[256]{0:T(256)S(1)} %get-tuple-element.12), kind=kLoop, calls=%fused_computation.15 | loop fusion | flops 7340032 | bytes 8408064 | tf_op jit(solution)/shard_map/broadcast_in_dim | solution.py:76
  (21 shorter events, 0.4 us)
Async XLA Ops:
  7.2 6.4 %copy-start.4 = (u32[256]{0:T(256)S(1)}, u32[256]{0:T(256)}, u32[]{:S(2)}) copy-start(u32[256]{0:T(256)} %constant.40) | copy-start | bytes 3076
  7.2 7.7 %copy-start.3 = (s32[1,256]{1,0:T(1,128)S(1)}, s32[1,256]{1,0:T(1,128)}, u32[]{:S(2)}) copy-start(s32[1,256]{1,0:T(1,128)} %param.6) | copy-start | bytes 3076
  7.2 73.6 %all-reduce.5.cloned.1.call-start = ((), (), s32[]{:S(2)}) async-start(), calls=%async_computation.2 | async-start | bytes 524288
  13.5 188.9 %all-gather.4.cloned.1.call-start = ((), (), s32[]{:S(2)}) async-start(), calls=%async_computation.1 | async-start | bytes 4210688 | tf_op jit(solution)/shard_map/all_gather | solution.py:38
  209.6 3.5 %copy-start.2 = (s32[2]{0:T(128)S(1)}, s32[2]{0:T(128)}, u32[]{:S(2)}) copy-start(s32[2]{0:T(128)} %param.9) | copy-start | bytes 28
  214.5 29.4 %all-to-all-start = ((bf16[256,2,512]{2,1,0:T(2,128)(2,1)}), bf16[256,2,512]{2,1,0:T(2,128)(2,1)S(1)}, u32[]{:S(2)}, u32[]{:S(2)}) async-start(bf16[256,2,512]{2,1,0:T(2,128)(2,1)} %stack.2), calls=%async_computation | async-start | bytes 1048576 | tf_op jit(solution)/shard_map/all_to_all | solution.py:59
  227.5 32.6 %copy-start = (bf16[1,256,4096]{2,1,0:T(8,128)(2,1)S(1)}, bf16[1,256,4096]{2,1,0:T(8,128)(2,1)}, u32[]{:S(2)}) copy-start(bf16[1,256,4096]{2,1,0:T(8,128)(2,1)} %param.5) | copy-start | bytes 6291460
  227.5 32.6 %copy-start.1 = (f32[4096]{0:T(1024)S(1)}, f32[4096]{0:T(1024)}, u32[]{:S(2)}) copy-start(f32[4096]{0:T(1024)} %param.7) | copy-start | bytes 49156
Sparse Core Ops, SparseCore 0:
  13.7 67.1 all-reduce.4
  85.1 117.3 all-gather.3
